TPU v7x, 128 devices: a whole 4x4x4 slice. The times are simulated.
128 devices in a mesh: cfg: 2 (over y_hi), group: 16 (over y_lo, x, core), mp: 4 (over z).
Axes of the slice: x: 4, y: 4 (y_hi: 2, y_lo: 2; y = y_hi * 2 + y_lo), z: 4, core: 2. Of those that a mesh axis runs over, the one named last changes fastest.
Arguments:
- latents: float32 [16384, 64], P(('group', 'mp')), may hold values from -0.6 to 0.6
- text_hidden: bfloat16 [2, 8192, 3072], P('cfg', ('group', 'mp')), may hold values from -6 to 6
- w_img_in: bfloat16 [64, 3072], replicated, may hold values from -0.75 to 0.75
- w_img_qkv: bfloat16 [3072, 4608], P(None, 'mp'), may hold values from -1 to 1
- w_txt_kv: bfloat16 [3072, 3072], P(None, 'mp'), may hold values from -0.109375 to 0.109375
- q_gain: float32 [128], replicated, may hold values from 0.25 to 1.75
- k_gain: float32 [128], replicated, may hold values from 0.25 to 1.75
- w_out: bfloat16 [1536, 3072], replicated, may hold values from -1 to 1
- w_final: bfloat16 [3072, 64], replicated, may hold values from -0.109375 to 0.109375
- mod_img: float32 [8, 3, 3072], replicated, may hold values from -3 to 3
- mod_txt: float32 [8, 2, 3072], replicated, may hold values from -3 to 3
- mod_final: float32 [8, 2, 3072], replicated, may hold values from -3 to 3
- guide: float32 [16], replicated, may hold values from 1.5 to 5
- step_size: float32 [8], replicated, may hold values from 0.02 to 0.3
- img_len: int32 [16], replicated, may hold values from 1 to 1024, as said below
- txt_len: int32 [16], replicated, may hold values from 1 to 512, as said below
- split_flag: int32 [2, 16], replicated, may hold values from 0 to 1, as said below
- tstep: int32 [16], replicated, may hold values from 0 to 7
Outputs:
- velocity: float32 [2, 8192, 64], P('cfg', ('group', 'mp'))
- next_latents: float32 [2, 8192, 64], P('cfg', ('group', 'mp'))
Inputs may be any that keep to these rules, and one draw needn't show every extreme that they name: `img_len`: some group has exactly 1024 live image tokens. `txt_len`: some group has exactly 512 live text tokens. `split_flag`: entries [c, 2j] and [c, 2j + 1] are equal; at least one such pair carries 1 and at least one carries 0.
All inputs are finite; a program needn't handle non-finite values.
Results may differ from a plain program's by a relative error of at most 0.035.
Values may be sent and summed in bfloat16 or wider, within the bound.
A program may use at most 192 MiB of HBM per device.

v0:
```python
import jax
import jax.numpy as jnp
from jax import lax
from jax.sharding import PartitionSpec as P

HD = 128


def partner(value, axis, bit):
    mask = 2**bit
    pairs = [(source, source ^ mask) for source in range(lax.axis_size(axis))]
    return lax.ppermute(value, axis, pairs)


def layer_norm(values):
    center = values - jnp.mean(values, -1, keepdims=True)
    spread = jnp.mean(center * center, -1, keepdims=True)
    return center * lax.rsqrt(spread + 1e-06)


def head_norm(values, gain):
    return values * lax.rsqrt(jnp.mean(values * values, -1, keepdims=True) + 1e-06) * gain


def pick_entry(table, index):
    return lax.dynamic_index_in_dim(table, index, 0, keepdims=False)


def local(
    latents,
    text_hidden,
    w_img_in,
    w_img_qkv,
    w_txt_kv,
    q_gain,
    k_gain,
    w_out,
    w_final,
    mod_img,
    mod_txt,
    mod_final,
    guide,
    step_size,
    img_len,
    txt_len,
    split_flag,
    tstep,
):
    group_index = lax.axis_index("group")
    mp_index = lax.axis_index("mp")
    cfg_index = lax.axis_index("cfg")
    mp_count = lax.axis_size("mp")
    mate_index = jnp.bitwise_xor(group_index, 1)
    step_index = pick_entry(tstep, group_index)
    mod_rows = pick_entry(mod_img, step_index)
    text_rows = pick_entry(mod_txt, step_index)
    final_rows = pick_entry(mod_final, step_index)
    shard_rows = latents.shape[0]
    half_rows = shard_rows // 2
    full_img = shard_rows * mp_count
    full_txt = text_hidden.shape[1] * mp_count
    local_heads = w_img_qkv.shape[1] // (3 * HD)
    x_img = jnp.dot(latents.astype(jnp.bfloat16), w_img_in, preferred_element_type=jnp.float32)
    lat_full = lax.all_gather(latents.astype(jnp.bfloat16), "mp", axis=0, tiled=True)
    x_full = jnp.dot(lat_full, w_img_in, preferred_element_type=jnp.float32)
    img_full = (layer_norm(x_full) * (1.0 + mod_rows[1]) + mod_rows[0]).astype(jnp.bfloat16)
    txt_mod = (
        layer_norm(text_hidden[0].astype(jnp.float32)) * (1.0 + text_rows[1]) + text_rows[0]
    ).astype(jnp.bfloat16)
    txt_full = lax.all_gather(txt_mod, "mp", axis=0, tiled=True)
    qkv = jnp.dot(img_full, w_img_qkv, preferred_element_type=jnp.float32).reshape(
        full_img, local_heads, 3, HD
    )
    query = head_norm(qkv[:, :, 0], q_gain).astype(jnp.bfloat16)
    key_img = head_norm(qkv[:, :, 1], k_gain).astype(jnp.bfloat16)
    value_img = qkv[:, :, 2].astype(jnp.bfloat16)
    text_kv = jnp.dot(txt_full, w_txt_kv, preferred_element_type=jnp.float32).reshape(
        full_txt, local_heads, 2, HD
    )
    key_txt = head_norm(text_kv[:, :, 0], k_gain).astype(jnp.bfloat16)
    value_txt = text_kv[:, :, 1].astype(jnp.bfloat16)
    key_rows = jnp.concatenate([key_txt, key_img], axis=0)
    value_rows = jnp.concatenate([value_txt, value_img], axis=0)
    mate_keys, mate_values = partner((key_rows, value_rows), "group", 0)
    spots_txt = jnp.arange(full_txt, dtype=jnp.int32)
    spots_img = jnp.arange(full_img, dtype=jnp.int32)

    def live_rows(index):
        return jnp.concatenate(
            [spots_txt < pick_entry(txt_len, index), spots_img < pick_entry(img_len, index)]
        )

    flagged = pick_entry(pick_entry(split_flag, cfg_index), group_index) == 1
    live = jnp.concatenate([live_rows(group_index), live_rows(mate_index) & flagged])
    all_keys = jnp.concatenate([key_rows, mate_keys], axis=0)
    all_values = jnp.concatenate([value_rows, mate_values], axis=0)
    scores = jnp.einsum(
        "qhe,khe->hqk", query, all_keys, preferred_element_type=jnp.float32
    ) * HD ** (-0.5)
    scores = jnp.where(live[None, None, :], scores, -1e30)
    weights = jnp.exp(scores - jnp.max(scores, -1, keepdims=True))
    probs = (weights / jnp.sum(weights, -1, keepdims=True)).astype(jnp.bfloat16)
    mixed = jnp.einsum(
        "hqk,khe->qhe", probs, all_values, preferred_element_type=jnp.float32
    ).astype(jnp.bfloat16)
    mixed = mixed.reshape(full_img, local_heads * HD)
    mixed = lax.all_to_all(mixed, "mp", split_axis=0, concat_axis=1, tiled=True)
    attended = jnp.dot(mixed, w_out, preferred_element_type=jnp.float32)
    hidden = x_img + mod_rows[2] * attended
    final = (layer_norm(hidden) * (1.0 + final_rows[1]) + final_rows[0]).astype(jnp.bfloat16)
    own_velocity = jnp.dot(final, w_final, preferred_element_type=jnp.float32)
    scale = pick_entry(guide, group_index)
    other_velocity = partner(own_velocity.astype(jnp.bfloat16), "cfg", 0).astype(own_velocity.dtype)
    is_cond = cfg_index == 0
    cond_part = jnp.where(is_cond, own_velocity, other_velocity)
    uncond_part = jnp.where(is_cond, other_velocity, own_velocity)
    guided_all = uncond_part + scale * (cond_part - uncond_part)
    guided = lax.dynamic_slice_in_dim(guided_all, cfg_index * half_rows, half_rows, 0)
    row_place = (
        mp_index * shard_rows + cfg_index * half_rows + jnp.arange(half_rows, dtype=jnp.int32)
    )
    row_live = row_place < pick_entry(img_len, group_index)
    guided = jnp.where(row_live[:, None], guided, 0.0)
    start_rows = lax.dynamic_slice_in_dim(latents, cfg_index * half_rows, half_rows, 0)
    moved = start_rows - pick_entry(step_size, step_index) * guided
    return (guided[None], moved[None])


def solution(mesh):
    placed = (
        P(("group", "mp"), None),
        P("cfg", ("group", "mp"), None),
        P(),
        P(None, "mp"),
        P(None, "mp"),
        P(),
        P(),
        P(),
        P(),
        P(),
        P(),
        P(),
        P(),
        P(),
        P(),
        P(),
        P(),
        P(),
    )
    return jax.shard_map(
        local,
        mesh=mesh,
        in_specs=placed,
        out_specs=(P("cfg", ("group", "mp"), None), P("cfg", ("group", "mp"), None)),
        check_vma=False,
    )
```

profile of v0, /device:TPU:0, one launch (start us, length us, event | category | flops | bytes accessed | tf_op | source)
XLA Modules:
  0.0 161.9 jit_solution(1764503549173147141)
XLA Ops:
  7.2 1.3 dynamic_slice.48
  9.8 1.3 convert_reduce_fusion
  11.2 1.5 fusion.21
  13.3 1.5 dynamic-slice_add_fusion
  14.8 2.4 %fusion.24 = bf16[128,3072]{1,0:T(8,128)(2,1)} fusion(bf16[1,128,3072]{2,1,0:T(8,128)(2,1)} %param.19, f32[3072]{0:T(1024)S(1)} %bitcast.102, f32[3072]{0:T(1024)S(1)} %bitcast.103, f32[128]{0:T(128)S(1)} %add_rsqrt_fusion.5, f32[128]{0:T(128)S(1)} %broadcast_multiply_fusion.2), kind=kLoop, calls=%fused_computation.35 | loop fusion | flops 2359296 | bytes 1598464 | tf_op jit(solution)/shard_map/convert_element_type | solution.py:69
  17.9 13.3 %all_gather.7 = bf16[1024,64]{0,1:T(8,128)(2,1)S(1)} all-gather(bf16[256,64]{0,1:T(8,128)(2,1)S(1)} %convert_element_type.51), channel_id=1, replica_groups=mesh['cfg'=2,'group'=16,'mp'=4] {'mp'}, dimensions={0}, use_global_device_ids=true | all-gather | bytes 163840 | tf_op jit(solution)/shard_map/all_gather | solution.py:64
  31.1 6.4 %fusion.52 = (f32[1024]{0:T(1024)S(1)}, f32[1024,3072]{1,0:T(8,128)}) fusion(bf16[1024,64]{0,1:T(8,128)(2,1)S(1)} %all_gather.7, bf16[64,3072]{1,0:T(8,128)(2,1)S(1)} %copy-done), kind=kOutput, calls=%fused_computation.95 | convolution fusion | flops 405797888 | bytes 13111296 | tf_op jit(solution)/shard_map/dot_general | solution.py:65
  37.5 6.0 %multiply_reduce_fusion = f32[1024]{0:T(1024)S(1)} fusion(f32[1024,3072]{1,0:T(8,128)} %get-tuple-element.15, f32[1024]{0:T(1024)S(1)} %broadcast_multiply_fusion), kind=kLoop, calls=%fused_computation.10 | loop fusion | flops 9436160 | bytes 12591104 | tf_op jit(solution)/shard_map/reduce_sum | solution.py:17
  43.6 0.9 fusion.41
  44.5 1.0 constant_dynamic-slice_fusion
  45.5 14.3 %fusion.6 = f32[1024,1152]{0,1:T(8,128)S(1)} fusion(bf16[3072,1152]{1,0:T(8,128)(2,1)} %param.21, f32[1024,3072]{1,0:T(8,128)} %get-tuple-element.15, f32[3072]{0:T(1024)S(1)} %bitcast.108, f32[3072]{0:T(1024)S(1)} %bitcast.107, f32[1024]{0:T(1024)S(1)} %add_rsqrt_fusion.3, f32[1024]{0:T(1024)S(1)} %broadcast_multiply_fusion), kind=kOutput, calls=%fused_computation.11 | convolution fusion | flops 7263485952 | bytes 24412160 | tf_op jit(solution)/shard_map/dot_general | solution.py:71
  59.7 2.1 %copy-done.1 = f32[1024,1152]{0,1:T(8,128)} copy-done((f32[1024,1152]{0,1:T(8,128)}, f32[1024,1152]{0,1:T(8,128)S(1)}, u32[]{:S(2)}) %copy-start.1) | copy-done | bytes 4718616
  62.6 1.4 fusion.50
  65.2 0.7 iota_compare_fusion.1
  66.4 1.1 fusion.27
  67.6 7.3 %fusion.56 = f32[512,768]{1,0:T(8,128)} fusion(bf16[512,3072]{1,0:T(8,128)(2,1)} %all-gather.2.cloned.1.call-done, bf16[3072,768]{1,0:T(8,128)(2,1)} %param.22), kind=kOutput, calls=%fused_computation.99 | convolution fusion | flops 2415919104 | bytes 9437184 | tf_op jit(solution)/shard_map/dot_general | solution.py:77
  74.9 2.1 %reshape.127 = f32[512,3,2,128]{3,2,1,0:T(2,128)S(1)} reshape(f32[512,768]{1,0:T(8,128)} %fusion.56) | data formatting | bytes 3145728 | tf_op jit(solution)/shard_map/reshape | solution.py:77
  78.2 1.1 pad_maximum_fusion.2
  81.3 1.6 multiply_reduce_fusion.2
  83.5 1.5 fusion.36
  85.0 0.8 slice.57
  85.8 1.0 copy.42
  87.5 19.3 %fusion.53 = (f32[3,1024]{1,0:T(4,128)S(1)}, f32[3,1024,3072]{2,1,0:T(8,128)}) fusion(pred[3072]{0:T(1024)(128)(4,1)S(1)} %pad_add_fusion, bf16[1536,3,128]{2,0,1:T(8,128)(2,1)} %collective-permute-done.1, bf16[1024,3,128]{2,0,1:T(8,128)(2,1)} %copy-done.2, bf16[512,3,128]{2,0,1:T(8,128)(2,1)} %copy-done.3, f32[1024,3,3,128]{0,3,2,1:T(8,128)} %bitcast.99, ...), kind=kOutput, calls=%fused_computation.96 | convolution fusion | flops 2461928448 | bytes 41713152 | tf_op jit(solution)/shard_map/sub | solution.py:101
  106.8 14.9 %fusion.32 = bf16[1024,3,128]{0,2,1:T(8,128)(2,1)S(1)} fusion(f32[3,1024,3072]{2,1,0:T(8,128)} %get-tuple-element.17, f32[3,1024]{1,0:T(4,128)S(1)} %get-tuple-element.16, bf16[1536,3,128]{0,2,1:T(8,128)(2,1)} %collective-permute-done, bf16[1024,3,128]{0,2,1:T(8,128)(2,1)S(1)} %fusion.36, bf16[512,3,128]{0,2,1:T(8,128)(2,1)S(1)} %bitcast.101), kind=kOutput, calls=%fused_computation.47 | convolution fusion | flops 2442264576 | bytes 40906752 | tf_op jit(solution)/shard_map/hqk,khe->qhe/dot_general | solution.py:103
  122.3 1.0 copy.33
  123.2 4.3 %all-to-all-start = ((bf16[4,256,384]{1,2,0:T(8,128)(2,1)}), bf16[4,256,384]{1,2,0:T(8,128)(2,1)S(1)}, u32[]{:S(2)}, u32[]{:S(2)}) async-start(bf16[4,256,384]{1,2,0:T(8,128)(2,1)} %copy.33), calls=%async_computation | async-start | bytes 1572864 | tf_op jit(solution)/shard_map/all_to_all | solution.py:107
  127.5 12.5 %all-to-all-done = bf16[4,256,384]{1,2,0:T(8,128)(2,1)S(1)} async-done(((bf16[4,256,384]{1,2,0:T(8,128)(2,1)}), bf16[4,256,384]{1,2,0:T(8,128)(2,1)S(1)}, u32[]{:S(2)}, u32[]{:S(2)}) %all-to-all-start) | async-done | bytes 786464 | tf_op jit(solution)/shard_map/all_to_all | solution.py:107
  140.0 5.2 %convolution_multiply_fusion = f32[256,3072]{1,0:T(8,128)S(1)} fusion(bf16[256,1536]{0,1:T(8,128)(2,1)S(1)} %bitcast.95, bf16[1536,3072]{1,0:T(8,128)(2,1)} %param.25, f32[3072]{0:T(1024)S(1)} %bitcast.104), kind=kOutput, calls=%fused_computation.18 | convolution fusion | flops 2416705536 | bytes 13381632 | tf_op jit(solution)/shard_map/dot_general | solution.py:108
  146.9 0.7 fusion.55
  147.7 3.3 %collective-permute-start.2 = (bf16[256,64]{0,1:T(8,128)(2,1)S(1)}, bf16[256,64]{0,1:T(8,128)(2,1)S(1)}, u32[]{:S(2)}, u32[]{:S(2)}) collective-permute-start(bf16[256,64]{0,1:T(8,128)(2,1)S(1)} %get-tuple-element.20), channel_id=1, source_target_pairs={{0,64},{64,0},{1,65},{65,1},{2,66},{66,2},{3,67},{67,3},{4,68},{68... | collective-permute-start | bytes 98312 | tf_op jit(solution)/shard_map/ppermute | solution.py:12
  151.0 0.7 add_compare_fusion
  153.2 1.9 %subtract_bitcast_fusion = (f32[1,128,64]{1,2,0:T(8,128)}, f32[1,128,64]{1,2,0:T(8,128)}) fusion(f32[256,64]{0,1:T(8,128)S(1)} %copy-done.7, s32[]{:T(128)S(6)} %select_n.65, f32[]{:T(128)} %bitcast.25, f32[]{:T(128)} %bitcast.23, f32[256,64]{0,1:T(8,128)S(1)} %get-tuple-element.21, bf16[256,64]{0,1:T(8,128)(2,1)S(1)} %collective-permute-done.2, pred[]{:T(512)S(6)} %eq.9, ...), kind=kLoop, calls=%fused_computation.62 | loop fusion | flops 73728 | bytes 147597 | tf_op jit(solution)/shard_map/broadcast_in_dim | solution.py:126
  (67 shorter events, 10.5 us)
Async XLA Ops:
  7.2 24.0 %copy-start = (bf16[64,3072]{1,0:T(8,128)(2,1)S(1)}, bf16[64,3072]{1,0:T(8,128)(2,1)}, u32[]{:S(2)}) copy-start(bf16[64,3072]{1,0:T(8,128)(2,1)} %param.20) | copy-start | bytes 1179652
  7.2 10.0 %copy-start.6 = (f32[256,64]{0,1:T(8,128)S(1)}, f32[256,64]{0,1:T(8,128)}, u32[]{:S(2)}) copy-start(f32[256,64]{0,1:T(8,128)} %param.18) | copy-start | bytes 196612
  7.2 60.4 %all-gather.2.cloned.1.call-start = ((), (), s32[]{:S(2)}) async-start(), calls=%async_computation.1 | async-start | bytes 3932160 | tf_op jit(solution)/shard_map/all_gather | solution.py:70
  17.2 0.6 copy-start.4
  59.7 2.2 %copy-start.1 = (f32[1024,1152]{0,1:T(8,128)}, f32[1024,1152]{0,1:T(8,128)S(1)}, u32[]{:S(2)}) copy-start(f32[1024,1152]{0,1:T(8,128)S(1)} %fusion.6) | copy-start | bytes 14155780
  61.9 0.7 copy-start.10
  67.6 10.6 %copy-start.2 = (bf16[1024,3,128]{2,0,1:T(8,128)(2,1)}, bf16[1024,3,128]{2,0,1:T(8,128)(2,1)S(1)}, u32[]{:S(2)}) copy-start(bf16[1024,3,128]{2,0,1:T(8,128)(2,1)S(1)} %fusion.27) | copy-start | bytes 2359300
  74.9 3.0 %copy-start.11 = (f32[128]{0:T(128)S(1)}, f32[128]{0:T(128)}, u32[]{:S(2)}) copy-start(f32[128]{0:T(128)} %param.24) | copy-start | bytes 1540
  77.0 3.0 %copy-start.12 = (s32[2,16]{1,0:T(2,128)S(1)}, s32[2,16]{1,0:T(2,128)}, u32[]{:S(2)}) copy-start(s32[2,16]{1,0:T(2,128)} %param.34) | copy-start | bytes 388
  78.2 1.2 copy-start.3
  79.3 8.2 %collective-permute-start.1 = (bf16[1536,3,128]{2,0,1:T(8,128)(2,1)}, bf16[1536,3,128]{2,0,1:T(8,128)(2,1)}, u32[]{:S(2)}, u32[]{:S(2)}) collective-permute-start(bf16[1536,3,128]{2,0,1:T(8,128)(2,1)} %pad_maximum_fusion.2), channel_id=1, source_target_pairs={{0,4},{4,0},{8,12},{12,8},{16,20},{20,16},{24,28},{28,24},{32,36},... | collective-permute-start | bytes 3538952 | tf_op jit(solution)/shard_map/ppermute | solution.py:12
  86.9 19.9 %collective-permute-start = (bf16[1536,3,128]{0,2,1:T(8,128)(2,1)S(1)}, bf16[1536,3,128]{0,2,1:T(8,128)(2,1)}, u32[]{:S(2)}, u32[]{:S(2)}) collective-permute-start(bf16[1536,3,128]{0,2,1:T(8,128)(2,1)S(1)} %pad_maximum_fusion.1), channel_id=1, source_target_pairs={{0,4},{4,0},{8,12},{12,8},{16,20},{20,16},{24,28},{28,24},{32,36},... | collective-permute-start | bytes 3538952 | tf_op jit(solution)/shard_map/ppermute | solution.py:12
  123.2 16.7 %all-to-all-start = ((bf16[4,256,384]{1,2,0:T(8,128)(2,1)}), bf16[4,256,384]{1,2,0:T(8,128)(2,1)S(1)}, u32[]{:S(2)}, u32[]{:S(2)}) async-start(bf16[4,256,384]{1,2,0:T(8,128)(2,1)} %copy.33), calls=%async_computation | async-start | bytes 1572864 | tf_op jit(solution)/shard_map/all_to_all | solution.py:107
  140.0 5.2 %copy-start.5 = (bf16[256,64]{0,1:T(8,128)(2,1)S(1)}, bf16[256,64]{0,1:T(8,128)(2,1)}, u32[]{:S(2)}) copy-start(bf16[256,64]{0,1:T(8,128)(2,1)} %copy-done.4) | copy-start | bytes 98308
  145.9 0.7 copy-start.8
  145.9 0.7 copy-start.9
  145.9 1.0 copy-start.13
  145.9 5.7 %copy-start.14 = (f32[8]{0:T(128)S(1)}, f32[8]{0:T(128)}, u32[]{:S(2)}) copy-start(f32[8]{0:T(128)} %param.31) | copy-start | bytes 100
  145.9 6.4 %copy-start.15 = (f32[16]{0:T(128)S(1)}, f32[16]{0:T(128)}, u32[]{:S(2)}) copy-start(f32[16]{0:T(128)} %param.30) | copy-start | bytes 196
  145.9 7.2 %copy-start.7 = (f32[256,64]{0,1:T(8,128)S(1)}, f32[256,64]{0,1:T(8,128)}, u32[]{:S(2)}) copy-start(f32[256,64]{0,1:T(8,128)} %param.18) | copy-start | bytes 196612
  147.7 5.5 %collective-permute-start.2 = (bf16[256,64]{0,1:T(8,128)(2,1)S(1)}, bf16[256,64]{0,1:T(8,128)(2,1)S(1)}, u32[]{:S(2)}, u32[]{:S(2)}) collective-permute-start(bf16[256,64]{0,1:T(8,128)(2,1)S(1)} %get-tuple-element.20), channel_id=1, source_target_pairs={{0,64},{64,0},{1,65},{65,1},{2,66},{66,2},{3,67},{67,3},{4,68},{68... | collective-permute-start | bytes 98312 | tf_op jit(solution)/shard_map/ppermute | solution.py:12
Sparse Core Ops, SparseCore 0:
  17.3 42.2 all-gather.1
where the time goes:
time: 163 us; the launch traced here: 162 us
  matrix products  68.8 us (42%)
  other arithmetic  24.9 us (15%)
  between operations  17.1 us (10%)
  local copies, waits for them, and re-layouts  17 us (10%)
  blocking collectives  13.3 us (8%)
  waiting for transfers between devices  12.8 us (8%)
  starting transfers between devices  8.17 us (5%)
    sub x1, matrix products, local(): weights = jnp.exp(scores - jnp.max(scores, -1, keepdims=True))  19.3 us
    dot_general x1, matrix products, local(): jnp.einsum('hqk,khe->qhe', probs, all_values, preferred_element_type=jnp....  14.9 us
    dot_general x1, matrix products, local(): jnp.dot(img_full, w_img_qkv, preferred_element_type=jnp.float32)  14.3 us
    all_gather x1, blocking collectives, local(): lax.all_gather(latents.astype(jnp.bfloat16), 'mp', axis=0, tiled=True)  13.3 us
    all_to_all x1, waiting for transfers between devices, local(): mixed = lax.all_to_all(mixed, 'mp', split_axis=0, concat_axis=1, tiled=True)  12.5 us
    reduce_sum x3, other arithmetic, layer_norm(): spread = jnp.mean(center * center, -1, keepdims=True)  7.98 us
    dot_general x1, matrix products, local(): jnp.dot(txt_full, w_txt_kv, preferred_element_type=jnp.float32)  7.3 us
    dot_general x1, matrix products, local(): x_full = jnp.dot(lat_full, w_img_in, preferred_element_type=jnp.float32)  6.4 us
  transfers between devices with their start and end apart: 5, of which 2 were waited for; matrix products, arithmetic and copies ran while one was open for 38% of the time, Pallas kernels for 0%

commit v1 on v0

--- a/solution.py
+++ b/solution.py
@@ -61,7 +61,25 @@
     full_txt = text_hidden.shape[1] * mp_count
     local_heads = w_img_qkv.shape[1] // (3 * HD)
     x_img = jnp.dot(latents.astype(jnp.bfloat16), w_img_in, preferred_element_type=jnp.float32)
-    lat_full = lax.all_gather(latents.astype(jnp.bfloat16), "mp", axis=0, tiled=True)
+    x = latents.astype(jnp.bfloat16)
+    size, position, extent = (lax.axis_size("mp"), lax.axis_index("mp"), x.shape[0])
+    upward = [(i, (i + 1) % size) for i in range(size)]
+    behind = [(i, (i - 1) % size) for i in range(size)]
+    out = jnp.zeros((*x.shape[:0], size * extent, *x.shape[0 + 1 :]), x.dtype)
+    out = lax.dynamic_update_slice_in_dim(out, x, position * extent, axis=0)
+    from_left = from_right = x
+    halfway = size // 2
+    for step in range(1, halfway + 1):
+        from_left = lax.ppermute(from_left, "mp", upward)
+        out = lax.dynamic_update_slice_in_dim(
+            out, from_left, (position - step) % size * extent, axis=0
+        )
+        if step < size - halfway:
+            from_right = lax.ppermute(from_right, "mp", behind)
+            out = lax.dynamic_update_slice_in_dim(
+                out, from_right, (position + step) % size * extent, axis=0
+            )
+    lat_full = out
     x_full = jnp.dot(lat_full, w_img_in, preferred_element_type=jnp.float32)
     img_full = (layer_norm(x_full) * (1.0 + mod_rows[1]) + mod_rows[0]).astype(jnp.bfloat16)
     txt_mod = (

time: 163 us -> 157 us (0.963)
  blocking collectives: 13.3 us -> 0 us
  waiting for transfers between devices: 12.8 us -> 23.1 us
  matrix products: 68.8 us -> 63.8 us
  starting transfers between devices: 8.17 us -> 11.5 us
  other arithmetic: 24.9 us -> 21.7 us
  local copies, waits for them, and re-layouts: 17 us -> 18.7 us
    all_gather x1 -> x0, blocking collectives: 13.3 us -> none  [local(): lax.all_gather(latents.astype(jnp.bfloat16), 'mp', axis=0, tiled=True)]
    ppermute x0 -> x3, waiting for transfers between devices: none -> 5.09 us  [the longest x2 5.09 us: local(): from_left = lax.ppermute(from_left, 'mp', upward)]
    all_gather x1, waiting for transfers between devices: 0.02 us -> 4.7 us  [local(): txt_full = lax.all_gather(txt_mod, 'mp', axis=0, tiled=True)]
    reduce_sum x3, other arithmetic: 7.98 us -> 3.32 us  [layer_norm(): spread = jnp.mean(center * center, -1, keepdims=True)]
    dot_general x1, matrix products: 6.4 us -> 1.9 us  [local(): x_full = jnp.dot(lat_full, w_img_in, preferred_element_type=jnp.float32)]
    ppermute x0 -> x3, starting transfers between devices: none -> 4.27 us  [the longest x1 2.2 us: local(): from_right = lax.ppermute(from_right, 'mp', behind)]
    unnamed x34 -> x42, local copies, waits for them, and re-layouts: 4.78 us -> 7.33 us
  transfers between devices with their start and end apart: 5 -> 8, of which waited for: 2 -> 4; matrix products, arithmetic and copies ran while one was open for 38% -> 39% of each run, Pallas kernels for 0% -> 0%
where the time goes in v1:
time: 157 us; the launch traced here: 156 us
  matrix products  63.8 us (41%)
  waiting for transfers between devices  23.1 us (15%)
  other arithmetic  21.7 us (14%)
  local copies, waits for them, and re-layouts  18.7 us (12%)
  between operations  17.1 us (11%)
  starting transfers between devices  11.5 us (7%)
    sub x1, matrix products, local(): weights = jnp.exp(scores - jnp.max(scores, -1, keepdims=True))  19.3 us
    dot_general x1, matrix products, local(): jnp.einsum('hqk,khe->qhe', probs, all_values, preferred_element_type=jnp....  14.8 us
    dot_general x1, matrix products, local(): jnp.dot(img_full, w_img_qkv, preferred_element_type=jnp.float32)  14.1 us
    all_to_all x1, waiting for transfers between devices, local(): mixed = lax.all_to_all(mixed, 'mp', split_axis=0, concat_axis=1, tiled=True)  12.7 us
    unnamed x42, local copies, waits for them, and re-layouts  7.33 us
    dot_general x1, matrix products, local(): jnp.dot(txt_full, w_txt_kv, preferred_element_type=jnp.float32)  7.04 us
    dot_general x1, matrix products, local(): attended = jnp.dot(mixed, w_out, preferred_element_type=jnp.float32)  5.21 us
    ppermute x2, waiting for transfers between devices, local(): from_left = lax.ppermute(from_left, 'mp', upward)  5.09 us
  transfers between devices with their start and end apart: 8, of which 4 were waited for; matrix products, arithmetic and copies ran while one was open for 39% of the time, Pallas kernels for 0%

profile of v1, /device:TPU:0, one launch (start us, length us, event | category | flops | bytes accessed | tf_op | source)
XLA Modules:
  0.0 156.0 jit_solution(8843302015684519553)
XLA Ops:
  8.1 2.1 %collective-permute-start = (bf16[256,64]{0,1:T(8,128)(2,1)S(1)}, bf16[256,64]{0,1:T(8,128)(2,1)S(1)}, u32[]{:S(2)}, u32[]{:S(2)}) collective-permute-start(bf16[256,64]{0,1:T(8,128)(2,1)S(1)} %get-tuple-element.3), channel_id=1, source_target_pairs={{0,1},{1,2},{2,3},{3,0},{4,5},{5,6},{6,7},{7,4},{8,9},{9,10},{10,1... | collective-permute-start | bytes 98312 | tf_op jit(solution)/shard_map/ppermute | solution.py:73
  10.2 2.2 %collective-permute-start.1 = (bf16[256,64]{0,1:T(8,128)(2,1)S(1)}, bf16[256,64]{0,1:T(8,128)(2,1)S(1)}, u32[]{:S(2)}, u32[]{:S(2)}) collective-permute-start(bf16[256,64]{0,1:T(8,128)(2,1)S(1)} %get-tuple-element.3), channel_id=1, source_target_pairs={{0,3},{1,0},{2,1},{3,2},{4,7},{5,4},{6,5},{7,6},{8,11},{9,8},{10,9... | collective-permute-start | bytes 98312 | tf_op jit(solution)/shard_map/ppermute | solution.py:78
  12.4 1.2 dynamic_slice.48
  14.9 1.3 convert_reduce_fusion
  16.3 1.5 fusion.21
  18.4 1.5 dynamic-slice_add_fusion
  19.9 2.4 %fusion.24 = bf16[128,3072]{1,0:T(8,128)(2,1)} fusion(bf16[1,128,3072]{2,1,0:T(8,128)(2,1)} %param.19, f32[3072]{0:T(1024)S(1)} %bitcast.102, f32[3072]{0:T(1024)S(1)} %bitcast.103, f32[128]{0:T(128)S(1)} %add_rsqrt_fusion.5, f32[128]{0:T(128)S(1)} %broadcast_multiply_fusion.2), kind=kLoop, calls=%fused_computation.35 | loop fusion | flops 2359296 | bytes 1598464 | tf_op jit(solution)/shard_map/convert_element_type | solution.py:87
  23.3 1.0 constant_dynamic-slice_fusion
  24.9 1.2 iota_compare_fusion
  26.1 1.1 iota_compare_fusion.1
  27.2 1.1 iota_compare_fusion.2
  28.4 5.1 %collective-permute-done.2 = bf16[256,64]{0,1:T(8,128)(2,1)S(1)} collective-permute-done((bf16[256,64]{0,1:T(8,128)(2,1)S(1)}, bf16[256,64]{0,1:T(8,128)(2,1)S(1)}, u32[]{:S(2)}, u32[]{:S(2)}) %collective-permute-start.2) | collective-permute-done | bytes 32800 | tf_op jit(solution)/shard_map/ppermute | solution.py:73
  33.5 1.9 %fusion.52 = (f32[1024]{0:T(1024)S(1)}, f32[1024,3072]{1,0:T(8,128)S(1)}) fusion(bf16[1024,64]{0,1:T(8,128)(2,1)S(1)} %constant_dynamic-update-slice_fusion, bf16[64,3072]{1,0:T(8,128)(2,1)S(1)} %copy-done), kind=kOutput, calls=%fused_computation.99 | convolution fusion | flops 405797888 | bytes 13111296 | tf_op jit(solution)/shard_map/dot_general | solution.py:83
  35.4 1.4 multiply_reduce_fusion
  36.8 3.1 %copy-done.1 = f32[1024,3072]{1,0:T(8,128)} copy-done((f32[1024,3072]{1,0:T(8,128)}, f32[1024,3072]{1,0:T(8,128)S(1)}, u32[]{:S(2)}) %copy-start.1) | copy-done | bytes 12582936
  39.9 14.1 %fusion.6 = f32[1024,1152]{0,1:T(8,128)S(1)} fusion(bf16[3072,1152]{1,0:T(8,128)(2,1)} %param.21, f32[1024,3072]{1,0:T(8,128)} %copy-done.1, f32[3072]{0:T(1024)S(1)} %bitcast.108, f32[3072]{0:T(1024)S(1)} %bitcast.107, f32[1024]{0:T(1024)S(1)} %add_rsqrt_fusion.3, f32[1024]{0:T(1024)S(1)} %broadcast_multiply_fusion), kind=kOutput, calls=%fused_computation.11 | convolution fusion | flops 7263485952 | bytes 24412160 | tf_op jit(solution)/shard_map/dot_general | solution.py:89
  54.0 2.2 %copy-done.2 = f32[1024,1152]{0,1:T(8,128)} copy-done((f32[1024,1152]{0,1:T(8,128)}, f32[1024,1152]{0,1:T(8,128)S(1)}, u32[]{:S(2)}) %copy-start.2) | copy-done | bytes 4718616
  57.8 4.7 %all-gather.2.cloned.1.call-done = bf16[512,3072]{1,0:T(8,128)(2,1)} async-done(((bf16[128,3072]{1,0:T(8,128)(2,1)}), bf16[512,3072]{1,0:T(8,128)(2,1)}) %all-gather.2.cloned.1.call-update) | async-done | bytes 3145744 | tf_op jit(solution)/shard_map/all_gather | solution.py:88
  62.5 7.0 %fusion.56 = f32[512,768]{1,0:T(8,128)} fusion(bf16[512,3072]{1,0:T(8,128)(2,1)} %all-gather.2.cloned.1.call-done, bf16[3072,768]{1,0:T(8,128)(2,1)} %param.22), kind=kOutput, calls=%fused_computation.103 | convolution fusion | flops 2415919104 | bytes 9437184 | tf_op jit(solution)/shard_map/dot_general | solution.py:95
  69.6 2.1 %reshape.127 = f32[512,3,2,128]{3,2,1,0:T(2,128)S(1)} reshape(f32[512,768]{1,0:T(8,128)} %fusion.56) | data formatting | bytes 3145728 | tf_op jit(solution)/shard_map/reshape | solution.py:95
  72.9 1.2 pad_maximum_fusion.2
  75.9 1.6 %multiply_reduce_fusion.2 = f32[1024,3]{0,1:T(4,128)S(1)} fusion(f32[1024,3,3,128]{0,3,2,1:T(8,128)} %bitcast.97), kind=kLoop, calls=%fused_computation.44 | loop fusion | flops 783360 | bytes 1585152 | tf_op jit(solution)/shard_map/reduce_sum | solution.py:22
  78.1 1.5 fusion.36
  80.5 1.0 copy.42
  82.1 19.3 %fusion.53 = (f32[3,1024]{1,0:T(4,128)S(1)}, f32[3,1024,3072]{2,1,0:T(8,128)}) fusion(pred[3072]{0:T(1024)(128)(4,1)S(1)} %pad_add_fusion, bf16[1536,3,128]{2,0,1:T(8,128)(2,1)} %collective-permute-done.4, bf16[1024,3,128]{2,0,1:T(8,128)(2,1)} %copy-done.3, bf16[512,3,128]{2,0,1:T(8,128)(2,1)} %copy-done.4, f32[1024,3,3,128]{0,3,2,1:T(8,128)} %bitcast.99, ...), kind=kOutput, calls=%fused_computation.100 | convolution fusion | flops 2461928448 | bytes 41713152 | tf_op jit(solution)/shard_map/sub | solution.py:119
  101.5 14.8 %fusion.32 = bf16[1024,3,128]{0,2,1:T(8,128)(2,1)S(1)} fusion(f32[3,1024,3072]{2,1,0:T(8,128)} %get-tuple-element.19, f32[3,1024]{1,0:T(4,128)S(1)} %get-tuple-element.18, bf16[1536,3,128]{0,2,1:T(8,128)(2,1)} %collective-permute-done.3, bf16[1024,3,128]{0,2,1:T(8,128)(2,1)S(1)} %fusion.36, bf16[512,3,128]{0,2,1:T(8,128)(2,1)S(1)} %bitcast.101), kind=kOutput, calls=%fused_computation.47 | convolution fusion | flops 2442264576 | bytes 40906752 | tf_op jit(solution)/shard_map/hqk,khe->qhe/dot_general | solution.py:121
  116.9 1.0 copy.33
  117.9 3.5 %all-to-all-start = ((bf16[4,256,384]{1,2,0:T(8,128)(2,1)}), bf16[4,256,384]{1,2,0:T(8,128)(2,1)S(1)}, u32[]{:S(2)}, u32[]{:S(2)}) async-start(bf16[4,256,384]{1,2,0:T(8,128)(2,1)} %copy.33), calls=%async_computation | async-start | bytes 1572864 | tf_op jit(solution)/shard_map/all_to_all | solution.py:125
  121.4 12.7 %all-to-all-done = bf16[4,256,384]{1,2,0:T(8,128)(2,1)S(1)} async-done(((bf16[4,256,384]{1,2,0:T(8,128)(2,1)}), bf16[4,256,384]{1,2,0:T(8,128)(2,1)S(1)}, u32[]{:S(2)}, u32[]{:S(2)}) %all-to-all-start) | async-done | bytes 786464 | tf_op jit(solution)/shard_map/all_to_all | solution.py:125
  134.1 5.2 %convolution_multiply_fusion = f32[256,3072]{1,0:T(8,128)S(1)} fusion(bf16[256,1536]{0,1:T(8,128)(2,1)S(1)} %bitcast.95, bf16[1536,3072]{1,0:T(8,128)(2,1)} %param.25, f32[3072]{0:T(1024)S(1)} %bitcast.104), kind=kOutput, calls=%fused_computation.18 | convolution fusion | flops 2416705536 | bytes 13381632 | tf_op jit(solution)/shard_map/dot_general | solution.py:126
  141.8 3.1 %collective-permute-start.5 = (bf16[256,64]{0,1:T(8,128)(2,1)S(1)}, bf16[256,64]{0,1:T(8,128)(2,1)S(1)}, u32[]{:S(2)}, u32[]{:S(2)}) collective-permute-start(bf16[256,64]{0,1:T(8,128)(2,1)S(1)} %get-tuple-element.22), channel_id=1, source_target_pairs={{0,64},{64,0},{1,65},{65,1},{2,66},{66,2},{3,67},{67,3},{4,68},{68... | collective-permute-start | bytes 98312 | tf_op jit(solution)/shard_map/ppermute | solution.py:12
  147.3 1.9 %subtract_bitcast_fusion = (f32[1,128,64]{1,2,0:T(8,128)}, f32[1,128,64]{1,2,0:T(8,128)}) fusion(f32[256,64]{0,1:T(8,128)S(1)} %copy-done.5, s32[]{:T(128)S(6)} %select_n.99, f32[]{:T(128)} %bitcast.25, f32[]{:T(128)} %bitcast.23, f32[256,64]{0,1:T(8,128)S(1)} %get-tuple-element.23, bf16[256,64]{0,1:T(8,128)(2,1)S(1)} %collective-permute-done.5, ...), kind=kLoop, calls=%fused_computation.62 | loop fusion | flops 73728 | bytes 147597 | tf_op jit(solution)/shard_map/broadcast_in_dim | solution.py:144
  (84 shorter events, 14.0 us)
Async XLA Ops:
  7.2 26.3 %copy-start = (bf16[64,3072]{1,0:T(8,128)(2,1)S(1)}, bf16[64,3072]{1,0:T(8,128)(2,1)}, u32[]{:S(2)}) copy-start(bf16[64,3072]{1,0:T(8,128)(2,1)} %param.20) | copy-start | bytes 1179652
  7.2 17.1 %copy-start.11 = (s32[16]{0:T(128)S(1)}, s32[16]{0:T(128)}, u32[]{:S(2)}) copy-start(s32[16]{0:T(128)} %param.32) | copy-start | bytes 196
  7.2 17.1 %copy-start.10 = (s32[16]{0:T(128)S(1)}, s32[16]{0:T(128)}, u32[]{:S(2)}) copy-start(s32[16]{0:T(128)} %param.33) | copy-start | bytes 196
  7.2 55.3 %all-gather.2.cloned.1.call-start = ((), (), s32[]{:S(2)}) async-start(), calls=%async_computation.1 | async-start | bytes 3932160 | tf_op jit(solution)/shard_map/all_gather | solution.py:88
  8.1 27.2 %copy-start.6 = (bf16[256,64]{0,1:T(8,128)(2,1)}, bf16[256,64]{0,1:T(8,128)(2,1)S(1)}, u32[]{:S(2)}) copy-start(bf16[256,64]{0,1:T(8,128)(2,1)S(1)} %get-tuple-element.3) | copy-start | bytes 98308
  8.1 20.2 %collective-permute-start = (bf16[256,64]{0,1:T(8,128)(2,1)S(1)}, bf16[256,64]{0,1:T(8,128)(2,1)S(1)}, u32[]{:S(2)}, u32[]{:S(2)}) collective-permute-start(bf16[256,64]{0,1:T(8,128)(2,1)S(1)} %get-tuple-element.3), channel_id=1, source_target_pairs={{0,1},{1,2},{2,3},{3,0},{4,5},{5,6},{6,7},{7,4},{8,9},{9,10},{10,1... | collective-permute-start | bytes 98312 | tf_op jit(solution)/shard_map/ppermute | solution.py:73
  10.2 18.1 %collective-permute-start.1 = (bf16[256,64]{0,1:T(8,128)(2,1)S(1)}, bf16[256,64]{0,1:T(8,128)(2,1)S(1)}, u32[]{:S(2)}, u32[]{:S(2)}) collective-permute-start(bf16[256,64]{0,1:T(8,128)(2,1)S(1)} %get-tuple-element.3), channel_id=1, source_target_pairs={{0,3},{1,0},{2,1},{3,2},{4,7},{5,4},{6,5},{7,6},{8,11},{9,8},{10,9... | collective-permute-start | bytes 98312 | tf_op jit(solution)/shard_map/ppermute | solution.py:78
  28.3 5.1 %collective-permute-start.2 = (bf16[256,64]{0,1:T(8,128)(2,1)S(1)}, bf16[256,64]{0,1:T(8,128)(2,1)S(1)}, u32[]{:S(2)}, u32[]{:S(2)}) collective-permute-start(bf16[256,64]{0,1:T(8,128)(2,1)S(1)} %collective-permute-done), channel_id=1, source_target_pairs={{0,1},{1,2},{2,3},{3,0},{4,5},{5,6},{6,7},{7,4},{8,9},{9,10},{10,1... | collective-permute-start | bytes 98312 | tf_op jit(solution)/shard_map/ppermute | solution.py:73
  35.4 4.5 %copy-start.1 = (f32[1024,3072]{1,0:T(8,128)}, f32[1024,3072]{1,0:T(8,128)S(1)}, u32[]{:S(2)}) copy-start(f32[1024,3072]{1,0:T(8,128)S(1)} %get-tuple-element.17) | copy-start | bytes 37748740
  54.0 2.2 %copy-start.2 = (f32[1024,1152]{0,1:T(8,128)}, f32[1024,1152]{0,1:T(8,128)S(1)}, u32[]{:S(2)}) copy-start(f32[1024,1152]{0,1:T(8,128)S(1)} %fusion.6) | copy-start | bytes 14155780
  56.3 1.0 copy-start.12
  57.8 15.0 %copy-start.3 = (bf16[1024,3,128]{2,0,1:T(8,128)(2,1)}, bf16[1024,3,128]{2,0,1:T(8,128)(2,1)S(1)}, u32[]{:S(2)}) copy-start(bf16[1024,3,128]{2,0,1:T(8,128)(2,1)S(1)} %fusion.27) | copy-start | bytes 2359300
  71.7 2.9 %copy-start.16 = (s32[2,16]{1,0:T(2,128)S(1)}, s32[2,16]{1,0:T(2,128)}, u32[]{:S(2)}) copy-start(s32[2,16]{1,0:T(2,128)} %param.34) | copy-start | bytes 388
  71.7 4.2 %copy-start.14 = (pred[1024]{0:T(1024)(128)(4,1)S(1)}, pred[1024]{0:T(1024)(128)(4,1)}, u32[]{:S(2)}) copy-start(pred[1024]{0:T(1024)(128)(4,1)} %iota_compare_fusion) | copy-start | bytes 3076
  71.7 4.2 %copy-start.15 = (pred[512]{0:T(512)(128)(4,1)S(1)}, pred[512]{0:T(512)(128)(4,1)}, u32[]{:S(2)}) copy-start(pred[512]{0:T(512)(128)(4,1)} %iota_compare_fusion.2) | copy-start | bytes 1540
  71.7 4.2 %copy-start.13 = (pred[1024]{0:T(1024)(128)(4,1)S(1)}, pred[1024]{0:T(1024)(128)(4,1)}, u32[]{:S(2)}) copy-start(pred[1024]{0:T(1024)(128)(4,1)} %iota_compare_fusion.1) | copy-start | bytes 3076
  72.9 1.2 copy-start.4
  74.0 8.1 %collective-permute-start.4 = (bf16[1536,3,128]{2,0,1:T(8,128)(2,1)}, bf16[1536,3,128]{2,0,1:T(8,128)(2,1)}, u32[]{:S(2)}, u32[]{:S(2)}) collective-permute-start(bf16[1536,3,128]{2,0,1:T(8,128)(2,1)} %pad_maximum_fusion.2), channel_id=1, source_target_pairs={{0,4},{4,0},{8,12},{12,8},{16,20},{20,16},{24,28},{28,24},{32,36},... | collective-permute-start | bytes 3538952 | tf_op jit(solution)/shard_map/ppermute | solution.py:12
  81.5 19.9 %collective-permute-start.3 = (bf16[1536,3,128]{0,2,1:T(8,128)(2,1)S(1)}, bf16[1536,3,128]{0,2,1:T(8,128)(2,1)}, u32[]{:S(2)}, u32[]{:S(2)}) collective-permute-start(bf16[1536,3,128]{0,2,1:T(8,128)(2,1)S(1)} %pad_maximum_fusion.1), channel_id=1, source_target_pairs={{0,4},{4,0},{8,12},{12,8},{16,20},{20,16},{24,28},{28,24},{32,36},... | collective-permute-start | bytes 3538952 | tf_op jit(solution)/shard_map/ppermute | solution.py:12
  117.9 16.2 %all-to-all-start = ((bf16[4,256,384]{1,2,0:T(8,128)(2,1)}), bf16[4,256,384]{1,2,0:T(8,128)(2,1)S(1)}, u32[]{:S(2)}, u32[]{:S(2)}) async-start(bf16[4,256,384]{1,2,0:T(8,128)(2,1)} %copy.33), calls=%async_computation | async-start | bytes 1572864 | tf_op jit(solution)/shard_map/all_to_all | solution.py:125
  134.1 5.2 %copy-start.7 = (bf16[256,64]{0,1:T(8,128)(2,1)S(1)}, bf16[256,64]{0,1:T(8,128)(2,1)}, u32[]{:S(2)}) copy-start(bf16[256,64]{0,1:T(8,128)(2,1)} %copy-done.6) | copy-start | bytes 98308
  140.0 0.7 copy-start.8
  140.0 0.7 copy-start.9
  140.0 1.0 copy-start.17
  140.1 5.4 %copy-start.18 = (f32[8]{0:T(128)S(1)}, f32[8]{0:T(128)}, u32[]{:S(2)}) copy-start(f32[8]{0:T(128)} %param.31) | copy-start | bytes 100
  140.1 6.0 %copy-start.19 = (f32[16]{0:T(128)S(1)}, f32[16]{0:T(128)}, u32[]{:S(2)}) copy-start(f32[16]{0:T(128)} %param.30) | copy-start | bytes 196
  140.1 7.2 %copy-start.5 = (f32[256,64]{0,1:T(8,128)S(1)}, f32[256,64]{0,1:T(8,128)}, u32[]{:S(2)}) copy-start(f32[256,64]{0,1:T(8,128)} %param.18) | copy-start | bytes 196612
  141.8 5.5 %collective-permute-start.5 = (bf16[256,64]{0,1:T(8,128)(2,1)S(1)}, bf16[256,64]{0,1:T(8,128)(2,1)S(1)}, u32[]{:S(2)}, u32[]{:S(2)}) collective-permute-start(bf16[256,64]{0,1:T(8,128)(2,1)S(1)} %get-tuple-element.22), channel_id=1, source_target_pairs={{0,64},{64,0},{1,65},{65,1},{2,66},{66,2},{3,67},{67,3},{4,68},{68... | collective-permute-start | bytes 98312 | tf_op jit(solution)/shard_map/ppermute | solution.py:12
Sparse Core Ops, SparseCore 0:
  22.4 40.0 all-gather.1
